TPU v7x, 32 devices: a whole 2x2x4 slice. The times are simulated.
32 devices in a mesh: seq: 4 (over x, core), grp: 8 (over z, y).
Axes of the slice: x: 2, y: 2, z: 4, core: 2. Of those that a mesh axis runs over, the one named last changes fastest.
Arguments:
- conv_input: bfloat16 [8, 512, 2688], P('grp', 'seq'), may hold values from -6 to 6
- conv_weight: float32 [4, 2688], replicated, may hold values from -3 to 3
- step_raw: float32 [8, 512, 40], P('grp', 'seq'), may hold values from -9 to 6
- rate_log: float32 [40], replicated, may hold values from -3 to 3.1
- skip_gain: float32 [40], replicated, may hold values from 0.5 to 1.5
- gate_input: bfloat16 [8, 512, 2560], P('grp', 'seq'), may hold values from -6 to 6
- norm_gain: float32 [2560], replicated, may hold values from 0.1 to 1.9
- out_weight: bfloat16 [2560, 2560], P('grp'), may hold values from -0.125 to 0.125
- residual: bfloat16 [8, 512, 2560], P('grp', 'seq'), may hold values from -6 to 6
- moe_gain: float32 [2560], replicated, may hold values from 0.1 to 1.9
- w_gate: bfloat16 [8, 2560, 512], P('grp'), may hold values from -0.125 to 0.125
- w_up: bfloat16 [8, 2560, 512], P('grp'), may hold values from -0.125 to 0.125
- w_down: bfloat16 [8, 512, 2560], P('grp'), may hold values from -0.25 to 0.25
- routes: int32 [8, 512, 2], P('grp', 'seq'), may hold values from 0 to 7, as said below
- route_weights: float32 [8, 512, 2], P('grp', 'seq'), may hold values from 0.2 to 1
Outputs:
- layer_out: bfloat16 [8, 512, 2560], P('grp', 'seq')
Inputs may be any that keep to these rules, and one draw needn't show every extreme that they name: `routes`: within the rows of one device (each aligned block of 128 frames of one manuscript) no expert is named by more than 64 entries, and one expert, the same in every block, is named by exactly 64; the two entries of a frame differ.
All inputs are finite; a program needn't handle non-finite values.
Results may differ from a plain program's by a relative error of at most 0.012.
Values may be sent and summed in bfloat16 or wider, within the bound.
A program may use at most 128 MiB of HBM per device.

v0:
```python
import jax
import jax.numpy as jnp
from jax import lax
from jax.sharding import PartitionSpec as P

EPSILON = 1e-05


def from_behind(value, axis, steps):
    count = lax.axis_size(axis)
    first, last = (max(0, -steps), min(count, count - steps))
    return lax.ppermute(value, axis, [(source, source + steps) for source in range(first, last)])


def on_device(
    conv_input,
    conv_weight,
    step_raw,
    rate_log,
    skip_gain,
    gate_input,
    norm_gain,
    out_weight,
    residual,
    moe_gain,
    w_gate,
    w_up,
    w_down,
    routes,
    route_weights,
):
    half = jnp.bfloat16
    ring = lax.axis_size("seq")
    own = lax.axis_index("seq")
    share = out_weight.shape[1] // ring
    weight_share = lax.all_gather(
        lax.dynamic_slice_in_dim(out_weight, own * share, share, axis=1), "grp", axis=0, tiled=True
    )
    frames_in = conv_input[0]
    row_count = frames_in.shape[0]
    tap_count = conv_weight.shape[0]
    channel_count = conv_weight.shape[1]
    head_count = rate_log.shape[0]
    inner_width = gate_input.shape[2]
    head_width = inner_width // head_count
    state_width = (channel_count - inner_width) // 2
    model_width = residual.shape[2]
    edge_rows = frames_in[row_count - (tap_count - 1) :]
    before = from_behind(edge_rows, "seq", 1)
    padded = jnp.concatenate([before, frames_in], axis=0).astype(jnp.float32)
    summed = conv_weight[0][None, :] * padded[0:row_count]
    for offset in range(1, tap_count):
        summed = summed + conv_weight[offset][None, :] * padded[offset : offset + row_count]
    signal = jax.nn.silu(summed).astype(jnp.bfloat16)
    x_part = signal[:, :inner_width]
    b_part = signal[:, inner_width : inner_width + state_width]
    c_part = signal[:, inner_width + state_width :]
    step_size = jax.nn.softplus(step_raw[0])
    log_decay = -step_size * jnp.exp(rate_log)[None, :]
    cumulative = jnp.cumsum(log_decay, axis=0)
    x_values = x_part.astype(jnp.float32).reshape(row_count, head_count, head_width)
    b_values = b_part.astype(jnp.float32)
    c_values = c_part.astype(jnp.float32)
    scores = jnp.dot(c_part, b_part.T, preferred_element_type=jnp.float32)
    positions = jnp.arange(row_count)
    causal = positions[:, None] >= positions[None, :]
    by_head = cumulative.T
    gap_log = by_head[:, :, None] - by_head[:, None, :]
    decay_mask = jnp.where(causal[None], jnp.exp(jnp.where(causal[None], gap_log, 0.0)), 0.0)
    mixing = (scores[None] * decay_mask * step_size.T[:, None, :]).astype(half)
    x_heads = x_part.reshape(row_count, head_count, head_width)
    tail_weight = jnp.exp(cumulative[-1][None, :] - cumulative) * step_size
    local_state = jnp.einsum(
        "shp,sn->hpn",
        (x_values * tail_weight[:, :, None]).astype(half),
        b_part,
        preferred_element_type=jnp.float32,
    ).astype(half)
    totals = lax.all_gather(cumulative[-1], "seq", axis=0)
    passing = jnp.zeros_like(totals[0])
    entering = jnp.zeros(local_state.shape, jnp.float32)
    for shift in range(1, ring):
        arrived_state = from_behind(local_state, "seq", shift).astype(jnp.float32)
        entering = entering + jnp.exp(passing)[:, None, None] * arrived_state
        passing = passing + totals[jnp.maximum(own - shift, 0)]
    within = jnp.einsum("hts,shp->thp", mixing, x_heads, preferred_element_type=jnp.float32)
    carried = (
        jnp.einsum("tn,hpn->thp", c_part, entering.astype(half), preferred_element_type=jnp.float32)
        * jnp.exp(cumulative)[:, :, None]
    )
    ssd_out = (within + carried + skip_gain[None, :, None] * x_values).reshape(
        row_count, inner_width
    )
    gated_out = ssd_out * jax.nn.silu(gate_input[0].astype(jnp.float32))
    mean_square = jnp.mean(gated_out * gated_out, axis=1, keepdims=True)
    normed = (gated_out * lax.rsqrt(mean_square + EPSILON) * norm_gain[None, :]).astype(
        jnp.bfloat16
    )
    all_rows = lax.all_gather(normed, "seq", axis=0, tiled=True)
    column_share = jnp.dot(all_rows, weight_share, preferred_element_type=jnp.float32).astype(half)
    projected = lax.all_to_all(column_share, "seq", split_axis=0, concat_axis=1, tiled=True).astype(
        jnp.float32
    )
    mixed_out = (residual[0].astype(jnp.float32) + projected).astype(jnp.bfloat16)
    mixed_float = mixed_out.astype(jnp.float32)
    mixed_square = jnp.mean(mixed_float * mixed_float, axis=1, keepdims=True)
    moe_in = (mixed_float * lax.rsqrt(mixed_square + EPSILON) * moe_gain[None, :]).astype(
        jnp.bfloat16
    )
    experts = lax.axis_size("grp")
    capacity = 4 * row_count // experts
    flat_picks = routes[0].reshape(-1)
    member = (flat_picks[:, None] == jnp.arange(experts)[None, :]).astype(jnp.int32)
    position = jnp.cumsum(member, axis=0) - member
    slot_index = jnp.sum(position * member, axis=1)
    target = (flat_picks * capacity + slot_index).reshape(row_count, 2)
    selector = jnp.any(
        target[None, :, :] == jnp.arange(experts * capacity)[:, None, None], axis=2
    ).astype(jnp.bfloat16)
    outgoing = (
        jnp.dot(selector, moe_in, preferred_element_type=jnp.float32)
        .astype(jnp.bfloat16)
        .reshape(experts, capacity, model_width)
    )
    gate_matrix = w_gate[0]
    up_matrix = w_up[0]
    down_matrix = w_down[0]
    arrived = lax.all_to_all(outgoing, "grp", split_axis=0, concat_axis=0, tiled=True)
    flattened_rows = arrived.reshape(-1, model_width)
    gate_part = jnp.dot(flattened_rows, gate_matrix, preferred_element_type=jnp.float32)
    up_part = jnp.dot(flattened_rows, up_matrix, preferred_element_type=jnp.float32)
    expert_hidden = (jax.nn.silu(gate_part) * up_part).astype(jnp.bfloat16)
    result = (
        jnp.dot(expert_hidden, down_matrix, preferred_element_type=jnp.float32)
        .astype(jnp.bfloat16)
        .reshape(arrived.shape)
    )
    returned = lax.all_to_all(result, "grp", split_axis=0, concat_axis=0, tiled=True)
    back_rows = returned.reshape(experts * capacity, model_width)
    slots = jnp.arange(experts * capacity)[None, :]
    first_pick = (target[:, 0:1] == slots).astype(half)
    second_pick = (target[:, 1:2] == slots).astype(half)
    first_out = jnp.dot(first_pick, back_rows, preferred_element_type=jnp.float32)
    second = jnp.dot(second_pick, back_rows, preferred_element_type=jnp.float32)
    pair_weights = route_weights[0]
    layer_out = mixed_float + pair_weights[:, 0:1] * first_out + pair_weights[:, 1:2] * second
    return layer_out.astype(jnp.bfloat16)[None]


def solution(mesh):
    in_specs = (
        P("grp", "seq", None),
        P(),
        P("grp", "seq", None),
        P(),
        P(),
        P("grp", "seq", None),
        P(),
        P("grp", None),
        P("grp", "seq", None),
        P(),
        P("grp", None, None),
        P("grp", None, None),
        P("grp", None, None),
        P("grp", "seq", None),
        P("grp", "seq", None),
    )
    out_specs = P("grp", "seq", None)
    return jax.shard_map(
        on_device, mesh=mesh, in_specs=in_specs, out_specs=out_specs, check_vma=False
    )
```

profile of v0, /device:TPU:0, one launch (start us, length us, event | category | flops | bytes accessed | tf_op | source)
XLA Modules:
  0.0 336.8 jit_solution(5236764994432943655)
XLA Ops:
  8.1 2.9 collective-permute-start
  15.1 5.7 %all-gather = f32[4,1,40]{2,1,0:T(1,128)S(1)} all-gather(f32[1,1,40]{2,1,0:T(1,128)S(1)} %get-tuple-element.13), channel_id=1, replica_groups=mesh['seq'=4,'grp'=8] {'seq'}, dimensions={0}, use_global_device_ids=true | all-gather | bytes 800 | tf_op jit(solution)/shard_map/all_gather | solution.py:79
  25.1 2.4 copy.79
  27.5 1.9 copy.71
  31.1 2.9 multiply_convert_fusion.1
  34.4 2.2 collective-permute-start.1
  36.6 3.3 collective-permute-start.2
  42.6 12.4 %collective-permute-done.2 = bf16[40,64,64]{2,1,0:T(8,128)(2,1)S(1)} collective-permute-done((bf16[40,64,64]{2,1,0:T(8,128)(2,1)S(1)}, bf16[40,64,64]{2,1,0:T(8,128)(2,1)S(1)}, u32[]{:S(2)}, u32[]{:S(2)}) %collective-permute-start.2) | collective-permute-done | bytes 327712 | tf_op jit(solution)/shard_map/ppermute | solution.py:12
  55.0 11.2 %collective-permute-done.3 = bf16[40,64,64]{2,1,0:T(8,128)(2,1)S(1)} collective-permute-done((bf16[40,64,64]{2,1,0:T(8,128)(2,1)S(1)}, bf16[40,64,64]{2,1,0:T(8,128)(2,1)S(1)}, u32[]{:S(2)}, u32[]{:S(2)}) %collective-permute-start.3) | collective-permute-done | bytes 327712 | tf_op jit(solution)/shard_map/ppermute | solution.py:12
  66.3 2.0 multiply_reduce_fusion
  68.3 2.9 copy.78
  71.1 2.6 fusion.33
  76.5 24.7 %all-gather.4.cloned.1.call-done = bf16[512,2560]{1,0:T(8,128)(2,1)} async-done(((bf16[128,2560]{1,0:T(8,128)(2,1)}), bf16[512,2560]{1,0:T(8,128)(2,1)}) %all-gather.4.cloned.1.call-update) | async-done | bytes 2621456 | tf_op jit(solution)/shard_map/all_gather | solution.py:99
  101.2 64.2 %all-gather.6.cloned.1.call-done = bf16[2560,640]{1,0:T(8,128)(2,1)} async-done(((bf16[320,640]{1,0:T(8,128)(2,1)}), bf16[2560,640]{1,0:T(8,128)(2,1)}) %all-gather.6.cloned.1.call-update) | async-done | bytes 3276816 | tf_op jit(solution)/shard_map/all_gather | solution.py:36
  165.4 5.7 %convolution_convert_fusion.2 = bf16[512,640]{1,0:T(8,128)(2,1)} fusion(bf16[512,2560]{1,0:T(8,128)(2,1)} %all-gather.4.cloned.1.call-done, bf16[2560,640]{1,0:T(8,128)(2,1)} %all-gather.6.cloned.1.call-done), kind=kOutput, calls=%fused_computation.32 | convolution fusion | flops 1678049280 | bytes 6553600 | tf_op jit(solution)/shard_map/dot_general | solution.py:100
  171.2 3.5 %all-to-all-start = ((bf16[4,128,640]{2,1,0:T(8,128)(2,1)}), bf16[4,128,640]{2,1,0:T(8,128)(2,1)S(1)}, u32[]{:S(2)}, u32[]{:S(2)}) async-start(bf16[4,128,640]{2,1,0:T(8,128)(2,1)} %bitcast.134), calls=%async_computation | async-start | bytes 1310720 | tf_op jit(solution)/shard_map/all_to_all | solution.py:101
  175.5 9.4 %all-to-all-done = bf16[4,128,640]{2,1,0:T(8,128)(2,1)S(1)} async-done(((bf16[4,128,640]{2,1,0:T(8,128)(2,1)}), bf16[4,128,640]{2,1,0:T(8,128)(2,1)S(1)}, u32[]{:S(2)}, u32[]{:S(2)}) %all-to-all-start) | async-done | bytes 655392 | tf_op jit(solution)/shard_map/all_to_all | solution.py:101
  187.3 62.7 %all_to_all.23 = bf16[8,64,2560]{2,1,0:T(8,128)(2,1)S(1)} all-to-all(bf16[8,64,2560]{2,1,0:T(8,128)(2,1)S(1)} %bitcast.123), channel_id=1, replica_groups=mesh['seq'=4,'grp'=8] {'grp'}, dimensions={0} | all-to-all | bytes 5242880 | tf_op jit(solution)/shard_map/all_to_all | solution.py:128
  251.5 2.5 fusion.7
  254.1 7.2 %convolution_convert_fusion = bf16[512,2560]{1,0:T(8,128)(2,1)} fusion(bf16[1,512,2560]{2,1,0:T(8,128)(2,1)S(1)} %copy-done, bf16[512,2560]{1,0:T(8,128)(2,1)} %bitcast.128, bf16[1,2560,512]{2,1,0:T(8,128)(2,1)} %param.26, f32[512,512]{1,0:T(8,128)} %fusion.7), kind=kOutput, calls=%fused_computation | convolution fusion | flops 2687238144 | bytes 11534336 | tf_op jit(solution)/shard_map/dot_general | solution.py:134
  261.3 4.5 %all-to-all-start.2 = ((bf16[8,64,2560]{2,1,0:T(8,128)(2,1)}), bf16[8,64,2560]{2,1,0:T(8,128)(2,1)}, u32[]{:S(2)}, u32[]{:S(2)}) async-start(bf16[8,64,2560]{2,1,0:T(8,128)(2,1)} %bitcast.126), calls=%async_computation.2 | async-start | bytes 5242880 | tf_op jit(solution)/shard_map/all_to_all | solution.py:138
  266.2 58.2 %all-to-all-done.2 = bf16[8,64,2560]{2,1,0:T(8,128)(2,1)} async-done(((bf16[8,64,2560]{2,1,0:T(8,128)(2,1)}), bf16[8,64,2560]{2,1,0:T(8,128)(2,1)}, u32[]{:S(2)}, u32[]{:S(2)}) %all-to-all-start.2) | async-done | bytes 2621472 | tf_op jit(solution)/shard_map/all_to_all | solution.py:138
  324.4 2.3 convolution_multiply_fusion
  326.7 3.2 fusion.3
  (83 shorter events, 22.3 us)
Async XLA Ops:
  6.5 247.5 %copy-start = (bf16[1,512,2560]{2,1,0:T(8,128)(2,1)S(1)}, bf16[1,512,2560]{2,1,0:T(8,128)(2,1)}, u32[]{:S(2)}) copy-start(bf16[1,512,2560]{2,1,0:T(8,128)(2,1)} %param.27) | copy-start | bytes 7864324
  6.5 94.7 %all-gather.4.cloned.1.call-start = ((), (), s32[]{:S(2)}) async-start(), calls=%async_computation.3 | async-start | bytes 3276800 | tf_op jit(solution)/shard_map/all_gather | solution.py:99
  8.1 19.4 %collective-permute-start = (bf16[3,2688]{1,0:T(4,128)(2,1)}, bf16[3,2688]{1,0:T(4,128)(2,1)}, u32[]{:S(2)}, u32[]{:S(2)}) collective-permute-start(bf16[3,2688]{1,0:T(4,128)(2,1)} %slice_bitcast_fusion), channel_id=1, source_target_pairs={{0,8},{8,16},{16,24},{1,9},{9,17},{17,25},{2,10},{10,18},{18,26},{... | collective-permute-start | bytes 48392 | tf_op jit(solution)/shard_map/ppermute | solution.py:12
  34.0 7.4 %copy-start.5 = (f32[40,128]{1,0:T(8,128)S(1)}, f32[40,128]{1,0:T(8,128)}, u32[]{:S(2)}) copy-start(f32[40,128]{1,0:T(8,128)} %copy.75) | copy-start | bytes 61444
  34.0 7.4 %copy-start.6 = (f32[40,128]{1,0:T(8,128)S(1)}, f32[40,128]{1,0:T(8,128)}, u32[]{:S(2)}) copy-start(f32[40,128]{1,0:T(8,128)} %copy.73) | copy-start | bytes 61444
  34.0 7.4 %copy-start.7 = (pred[128,128]{1,0:T(8,128)(4,1)S(1)}, pred[128,128]{1,0:T(8,128)(4,1)}, u32[]{:S(2)}) copy-start(pred[128,128]{1,0:T(8,128)(4,1)} %iota_compare_fusion.5) | copy-start | bytes 49156
  34.4 8.2 %collective-permute-start.1 = (bf16[40,64,64]{2,1,0:T(8,128)(2,1)S(1)}, bf16[40,64,64]{2,1,0:T(8,128)(2,1)S(1)}, u32[]{:S(2)}, u32[]{:S(2)}) collective-permute-start(bf16[40,64,64]{2,1,0:T(8,128)(2,1)S(1)} %convolution_convert_fusion.3), channel_id=1, source_target_pairs={{0,8},{8,16},{16,24},{1,9},{9,17},{17,25},{2,10},{10,18},{18,26},{... | collective-permute-start | bytes 983048 | tf_op jit(solution)/shard_map/ppermute | solution.py:12
  36.6 18.5 %collective-permute-start.2 = (bf16[40,64,64]{2,1,0:T(8,128)(2,1)S(1)}, bf16[40,64,64]{2,1,0:T(8,128)(2,1)S(1)}, u32[]{:S(2)}, u32[]{:S(2)}) collective-permute-start(bf16[40,64,64]{2,1,0:T(8,128)(2,1)S(1)} %convolution_convert_fusion.3), channel_id=1, source_target_pairs={{0,16},{8,24},{1,17},{9,25},{2,18},{10,26},{3,19},{11,27},{4,20},{... | collective-permute-start | bytes 983048 | tf_op jit(solution)/shard_map/ppermute | solution.py:12
  39.9 26.3 %collective-permute-start.3 = (bf16[40,64,64]{2,1,0:T(8,128)(2,1)S(1)}, bf16[40,64,64]{2,1,0:T(8,128)(2,1)S(1)}, u32[]{:S(2)}, u32[]{:S(2)}) collective-permute-start(bf16[40,64,64]{2,1,0:T(8,128)(2,1)S(1)} %convolution_convert_fusion.3), channel_id=1, source_target_pairs={{0,24},{1,25},{2,26},{3,27},{4,28},{5,29},{6,30},{7,31}} | collective-permute-start | bytes 983048 | tf_op jit(solution)/shard_map/ppermute | solution.py:12
  41.5 24.8 %copy-start.3 = (f32[1,128,2560]{1,2,0:T(8,128)S(1)}, f32[1,128,2560]{1,2,0:T(8,128)}, u32[]{:S(2)}) copy-start(f32[1,128,2560]{1,2,0:T(8,128)} %copy.79) | copy-start | bytes 3932164
  41.5 24.8 %copy-start.12 = (f32[40]{0:T(128)S(1)}, f32[40]{0:T(128)}, u32[]{:S(2)}) copy-start(f32[40]{0:T(128)} %get-tuple-element.18) | copy-start | bytes 484
  41.5 24.8 %copy-start.13 = (f32[40]{0:T(128)S(1)}, f32[40]{0:T(128)}, u32[]{:S(2)}) copy-start(f32[40]{0:T(128)} %get-tuple-element.19) | copy-start | bytes 484
  41.5 24.7 %copy-start.15 = (f32[40]{0:T(128)S(1)}, f32[40]{0:T(128)}, u32[]{:S(2)}) copy-start(f32[40]{0:T(128)} %param.19) | copy-start | bytes 484
  68.3 2.9 copy-start.2
  68.3 2.9 copy-start.8
  73.8 1.9 copy-start.10
  73.8 91.6 %all-gather.6.cloned.1.call-start = ((), (), s32[]{:S(2)}) async-start(), calls=%async_computation.4 | async-start | bytes 3686400 | tf_op jit(solution)/shard_map/all_gather | solution.py:36
  171.2 13.7 %all-to-all-start = ((bf16[4,128,640]{2,1,0:T(8,128)(2,1)}), bf16[4,128,640]{2,1,0:T(8,128)(2,1)S(1)}, u32[]{:S(2)}, u32[]{:S(2)}) async-start(bf16[4,128,640]{2,1,0:T(8,128)(2,1)} %bitcast.134), calls=%async_computation | async-start | bytes 1310720 | tf_op jit(solution)/shard_map/all_to_all | solution.py:101
  185.0 1.1 copy-start.4
  185.1 1.2 copy-start.9
  187.3 64.2 %copy-start.14 = (bf16[1,2560,512]{2,1,0:T(8,128)(2,1)S(1)}, bf16[1,2560,512]{2,1,0:T(8,128)(2,1)}, u32[]{:S(2)}) copy-start(bf16[1,2560,512]{2,1,0:T(8,128)(2,1)} %param.25) | copy-start | bytes 7864324
  250.0 1.5 copy-start.1
  261.3 4.9 %copy-start.11 = (f32[1,128,2]{1,2,0:T(2,128)S(1)}, f32[1,128,2]{1,2,0:T(2,128)}, u32[]{:S(2)}) copy-start(f32[1,128,2]{1,2,0:T(2,128)} %param.29) | copy-start | bytes 3076
  261.3 63.1 %all-to-all-start.2 = ((bf16[8,64,2560]{2,1,0:T(8,128)(2,1)}), bf16[8,64,2560]{2,1,0:T(8,128)(2,1)}, u32[]{:S(2)}, u32[]{:S(2)}) async-start(bf16[8,64,2560]{2,1,0:T(8,128)(2,1)} %bitcast.126), calls=%async_computation.2 | async-start | bytes 5242880 | tf_op jit(solution)/shard_map/all_to_all | solution.py:138
Sparse Core Ops, SparseCore 0:
  73.9 27.2 all-gather.3
  103.4 61.9 all-gather.5
where the time goes:
time: 338 us; the launch traced here: 337 us
  waiting for transfers between devices  180 us (53%)
  blocking collectives  68.3 us (20%)
  matrix products  25.6 us (8%)
  local copies, waits for them, and re-layouts  20.7 us (6%)
  starting transfers between devices  17.8 us (5%)
  between operations  13.7 us (4%)
  other arithmetic  10.4 us (3%)
    all_gather x1, waiting for transfers between devices, on_device(): lax.all_gather(lax.dynamic_slice_in_dim(out_weight, own * share, share, a...  64.2 us
    all_to_all x1, blocking collectives, on_device(): lax.all_to_all(outgoing, 'grp', split_axis=0, concat_axis=0, tiled=True)  62.7 us
    all_to_all x1, waiting for transfers between devices, on_device(): lax.all_to_all(result, 'grp', split_axis=0, concat_axis=0, tiled=True)  58.2 us
    all_gather x1, waiting for transfers between devices, on_device(): all_rows = lax.all_gather(normed, 'seq', axis=0, tiled=True)  24.7 us
    ppermute x4, waiting for transfers between devices, from_behind(): lax.ppermute(value, axis, [(source, source + steps) for source in range(f...  23.6 us
    ppermute x4, starting transfers between devices, from_behind(): lax.ppermute(value, axis, [(source, source + steps) for source in range(f...  9.76 us
    all_to_all x1, waiting for transfers between devices, on_device(): lax.all_to_all(column_share, 'seq', split_axis=0, concat_axis=1, tiled=True)  9.41 us
    dot_general x1, matrix products, on_device(): jnp.dot(expert_hidden, down_matrix, preferred_element_type=jnp.float32)  7.24 us
  transfers between devices with their start and end apart: 8, of which 6 were waited for; matrix products, arithmetic and copies ran while one was open for 5% of the time, Pallas kernels for 0%

commit v1 on v0

--- a/solution.py
+++ b/solution.py
@@ -1,9 +1,28 @@
+import functools
 import jax
 import jax.numpy as jnp
 from jax import lax
 from jax.sharding import PartitionSpec as P
 
 EPSILON = 1e-05
+
+
+def _trace_files(here_x, axis_no):
+    total_devices = lax.axis_size("seq")
+    column = tuple(((num, (num + 1) % total_devices) for num in range(total_devices)))
+
+    def pack_side_up(local_part):
+        if len(local_part) == total_devices:
+            return local_part
+        after = pack_side_up([lax.ppermute(local_part[0], "seq", perm=column), *local_part])
+        return after
+
+    state_next = jnp.concatenate(pack_side_up([here_x]), axis=axis_no)
+    low = jnp.roll(state_next, (lax.axis_index("seq") + 1) * here_x.shape[axis_no], axis=axis_no)
+    return low
+
+
+build_stacks_all_up = functools.partial(_trace_files, axis_no=0)
 
 
 def from_behind(value, axis, steps):
@@ -96,7 +115,7 @@
     normed = (gated_out * lax.rsqrt(mean_square + EPSILON) * norm_gain[None, :]).astype(
         jnp.bfloat16
     )
-    all_rows = lax.all_gather(normed, "seq", axis=0, tiled=True)
+    all_rows = build_stacks_all_up(normed)
     column_share = jnp.dot(all_rows, weight_share, preferred_element_type=jnp.float32).astype(half)
     projected = lax.all_to_all(column_share, "seq", split_axis=0, concat_axis=1, tiled=True).astype(
         jnp.float32

time: 338 us -> 292 us (0.86)
  waiting for transfers between devices: 180 us -> 121 us
  local copies, waits for them, and re-layouts: 20.7 us -> 31.6 us
    all_gather x1, waiting for transfers between devices: 64.2 us -> 0.01 us  [on_device(): lax.all_gather(lax.dynamic_slice_in_dim(out_weight, own * share, share, a...]
    ppermute x0 -> x3, waiting for transfers between devices: none -> 29.8 us  [pack_side_up(): lax.ppermute(local_part[0], 'seq', perm=column)]
    all_gather x1 -> x0, waiting for transfers between devices: 24.7 us -> none  [on_device(): all_rows = lax.all_gather(normed, 'seq', axis=0, tiled=True)]
    unnamed x36 -> x49, local copies, waits for them, and re-layouts: 4.92 us -> 15.6 us
  transfers between devices with their start and end apart: 8 -> 10, of which waited for: 6 -> 7; matrix products, arithmetic and copies ran while one was open for 5% -> 14% of each run, Pallas kernels for 0% -> 0%
where the time goes in v1:
time: 292 us; the launch traced here: 291 us
  waiting for transfers between devices  121 us (41%)
  blocking collectives  71.4 us (24%)
  local copies, waits for them, and re-layouts  31.6 us (11%)
  matrix products  25.6 us (9%)
  starting transfers between devices  17.8 us (6%)
  between operations  13.8 us (5%)
  other arithmetic  9.74 us (3%)
    all_to_all x1, blocking collectives, on_device(): lax.all_to_all(outgoing, 'grp', split_axis=0, concat_axis=0, tiled=True)  65.7 us
    all_to_all x1, waiting for transfers between devices, on_device(): lax.all_to_all(result, 'grp', split_axis=0, concat_axis=0, tiled=True)  58.2 us
    ppermute x3, waiting for transfers between devices, pack_side_up(): lax.ppermute(local_part[0], 'seq', perm=column)  29.8 us
    ppermute x4, waiting for transfers between devices, from_behind(): lax.ppermute(value, axis, [(source, source + steps) for source in range(f...  23.6 us
    unnamed x49, local copies, waits for them, and re-layouts  15.6 us
    ppermute x4, starting transfers between devices, from_behind(): lax.ppermute(value, axis, [(source, source + steps) for source in range(f...  9.75 us
    all_to_all x1, waiting for transfers between devices, on_device(): lax.all_to_all(column_share, 'seq', split_axis=0, concat_axis=1, tiled=True)  9.41 us
    dot_general x1, matrix products, on_device(): jnp.dot(expert_hidden, down_matrix, preferred_element_type=jnp.float32)  7.24 us
  transfers between devices with their start and end apart: 10, of which 7 were waited for; matrix products, arithmetic and copies ran while one was open for 14% of the time, Pallas kernels for 0%

profile of v1, /device:TPU:0, one launch (start us, length us, event | category | flops | bytes accessed | tf_op | source)
XLA Modules:
  0.0 291.0 jit_solution(4322513391719245790)
XLA Ops:
  8.1 2.9 %collective-permute-start = (bf16[3,2688]{1,0:T(4,128)(2,1)}, bf16[3,2688]{1,0:T(4,128)(2,1)}, u32[]{:S(2)}, u32[]{:S(2)}) collective-permute-start(bf16[3,2688]{1,0:T(4,128)(2,1)} %slice_bitcast_fusion), channel_id=1, source_target_pairs={{0,8},{8,16},{16,24},{1,9},{9,17},{17,25},{2,10},{10,18},{18,26},{... | collective-permute-start | bytes 48392 | tf_op jit(solution)/shard_map/ppermute | solution.py:31
  15.6 5.7 %all-gather = f32[4,1,40]{2,1,0:T(1,128)S(1)} all-gather(f32[1,1,40]{2,1,0:T(1,128)S(1)} %get-tuple-element.13), channel_id=1, replica_groups=mesh['seq'=4,'grp'=8] {'seq'}, dimensions={0}, use_global_device_ids=true | all-gather | bytes 800 | tf_op jit(solution)/shard_map/all_gather | solution.py:98
  25.7 2.4 copy.79
  31.6 2.9 multiply_convert_fusion.1
  35.0 2.1 collective-permute-start.1
  37.1 3.3 %collective-permute-start.2 = (bf16[40,64,64]{2,1,0:T(8,128)(2,1)S(1)}, bf16[40,64,64]{2,1,0:T(8,128)(2,1)S(1)}, u32[]{:S(2)}, u32[]{:S(2)}) collective-permute-start(bf16[40,64,64]{2,1,0:T(8,128)(2,1)S(1)} %convolution_convert_fusion.2), channel_id=1, source_target_pairs={{0,16},{8,24},{1,17},{9,25},{2,18},{10,26},{3,19},{11,27},{4,20},{... | collective-permute-start | bytes 983048 | tf_op jit(solution)/shard_map/ppermute | solution.py:31
  43.2 12.4 %collective-permute-done.2 = bf16[40,64,64]{2,1,0:T(8,128)(2,1)S(1)} collective-permute-done((bf16[40,64,64]{2,1,0:T(8,128)(2,1)S(1)}, bf16[40,64,64]{2,1,0:T(8,128)(2,1)S(1)}, u32[]{:S(2)}, u32[]{:S(2)}) %collective-permute-start.2) | collective-permute-done | bytes 327712 | tf_op jit(solution)/shard_map/ppermute | solution.py:31
  55.6 11.2 %collective-permute-done.3 = bf16[40,64,64]{2,1,0:T(8,128)(2,1)S(1)} collective-permute-done((bf16[40,64,64]{2,1,0:T(8,128)(2,1)S(1)}, bf16[40,64,64]{2,1,0:T(8,128)(2,1)S(1)}, u32[]{:S(2)}, u32[]{:S(2)}) %collective-permute-start.3) | collective-permute-done | bytes 327712 | tf_op jit(solution)/shard_map/ppermute | solution.py:31
  66.8 2.0 multiply_reduce_fusion
  68.8 2.8 copy.78
  73.6 10.2 %collective-permute-done.4 = bf16[128,2560]{1,0:T(8,128)(2,1)S(1)} collective-permute-done((bf16[128,2560]{1,0:T(8,128)(2,1)S(1)}, bf16[128,2560]{1,0:T(8,128)(2,1)S(1)}, u32[]{:S(2)}, u32[]{:S(2)}) %collective-permute-start.4) | collective-permute-done | bytes 655392 | tf_op jit(solution)/shard_map/ppermute | solution.py:17
  84.7 10.1 %collective-permute-done.5 = bf16[128,2560]{1,0:T(8,128)(2,1)} collective-permute-done((bf16[128,2560]{1,0:T(8,128)(2,1)S(1)}, bf16[128,2560]{1,0:T(8,128)(2,1)}, u32[]{:S(2)}, u32[]{:S(2)}) %collective-permute-start.5) | collective-permute-done | bytes 655392 | tf_op jit(solution)/shard_map/ppermute | solution.py:17
  95.6 9.5 %collective-permute-done.6 = bf16[128,2560]{1,0:T(8,128)(2,1)} collective-permute-done((bf16[128,2560]{1,0:T(8,128)(2,1)}, bf16[128,2560]{1,0:T(8,128)(2,1)}, u32[]{:S(2)}, u32[]{:S(2)}) %collective-permute-start.6) | collective-permute-done | bytes 655392 | tf_op jit(solution)/shard_map/ppermute | solution.py:17
  107.1 2.0 constant_dynamic-update-slice_fusion.6
  116.6 5.7 %fusion.19 = bf16[512,640]{1,0:T(8,128)(2,1)} fusion(bf16[2560,640]{1,0:T(8,128)(2,1)} %all-gather.3.cloned.1.call-done, bf16[1024,2560]{1,0:T(8,128)(2,1)} %constant_dynamic-update-slice_fusion, s32[]{:T(128)S(6)} %select_n.37), kind=kOutput, calls=%fused_computation.34 | convolution fusion | flops 1678049280 | bytes 6553604 | tf_op jit(solution)/shard_map/dot_general | solution.py:119
  122.3 3.5 %all-to-all-start = ((bf16[4,128,640]{2,1,0:T(8,128)(2,1)}), bf16[4,128,640]{2,1,0:T(8,128)(2,1)S(1)}, u32[]{:S(2)}, u32[]{:S(2)}) async-start(bf16[4,128,640]{2,1,0:T(8,128)(2,1)} %bitcast.133), calls=%async_computation | async-start | bytes 1310720 | tf_op jit(solution)/shard_map/all_to_all | solution.py:120
  126.6 9.4 %all-to-all-done = bf16[4,128,640]{2,1,0:T(8,128)(2,1)S(1)} async-done(((bf16[4,128,640]{2,1,0:T(8,128)(2,1)}), bf16[4,128,640]{2,1,0:T(8,128)(2,1)S(1)}, u32[]{:S(2)}, u32[]{:S(2)}) %all-to-all-start) | async-done | bytes 655392 | tf_op jit(solution)/shard_map/all_to_all | solution.py:120
  138.5 65.7 %all_to_all.23 = bf16[8,64,2560]{2,1,0:T(8,128)(2,1)S(1)} all-to-all(bf16[8,64,2560]{2,1,0:T(8,128)(2,1)S(1)} %bitcast.122), channel_id=1, replica_groups=mesh['seq'=4,'grp'=8] {'grp'}, dimensions={0} | all-to-all | bytes 5242880 | tf_op jit(solution)/shard_map/all_to_all | solution.py:147
  205.7 2.5 fusion.7
  208.3 7.2 %convolution_convert_fusion = bf16[512,2560]{1,0:T(8,128)(2,1)} fusion(bf16[1,512,2560]{2,1,0:T(8,128)(2,1)S(1)} %copy-done, bf16[512,2560]{1,0:T(8,128)(2,1)} %bitcast.127, bf16[1,2560,512]{2,1,0:T(8,128)(2,1)} %param.26, f32[512,512]{1,0:T(8,128)} %fusion.7), kind=kOutput, calls=%fused_computation | convolution fusion | flops 2687238144 | bytes 11534336 | tf_op jit(solution)/shard_map/dot_general | solution.py:153
  215.5 4.5 %all-to-all-start.2 = ((bf16[8,64,2560]{2,1,0:T(8,128)(2,1)}), bf16[8,64,2560]{2,1,0:T(8,128)(2,1)}, u32[]{:S(2)}, u32[]{:S(2)}) async-start(bf16[8,64,2560]{2,1,0:T(8,128)(2,1)} %bitcast.125), calls=%async_computation.2 | async-start | bytes 5242880 | tf_op jit(solution)/shard_map/all_to_all | solution.py:157
  220.4 58.2 %all-to-all-done.2 = bf16[8,64,2560]{2,1,0:T(8,128)(2,1)} async-done(((bf16[8,64,2560]{2,1,0:T(8,128)(2,1)}), bf16[8,64,2560]{2,1,0:T(8,128)(2,1)}, u32[]{:S(2)}, u32[]{:S(2)}) %all-to-all-start.2) | async-done | bytes 2621472 | tf_op jit(solution)/shard_map/all_to_all | solution.py:157
  278.6 2.3 convolution_multiply_fusion
  280.9 3.2 %fusion.3 = bf16[1,128,2560]{2,1,0:T(8,128)(2,1)} fusion(f32[128,2560]{1,0:T(8,128)S(1)} %convolution_multiply_fusion, bf16[512,2560]{1,0:T(8,128)(2,1)} %bitcast.31, bf16[128,2560]{1,0:T(8,128)(2,1)S(1)} %get-tuple-element.12, f32[128]{0:T(128)S(1)} %get-tuple-element.20, s32[128]{0:T(128)S(1)} %get-tuple-element.5), kind=kOutput, calls=%fused_computation.7 | convolution fusion | flops 337248256 | bytes 5243904 | tf_op jit(solution)/shard_map/dot_general | solution.py:162
  (100 shorter events, 35.2 us)
Async XLA Ops:
  6.5 201.7 %copy-start = (bf16[1,512,2560]{2,1,0:T(8,128)(2,1)S(1)}, bf16[1,512,2560]{2,1,0:T(8,128)(2,1)}, u32[]{:S(2)}) copy-start(bf16[1,512,2560]{2,1,0:T(8,128)(2,1)} %param.27) | copy-start | bytes 7864324
  6.5 8.0 %copy-start.6 = (f32[1,128,40]{1,2,0:T(8,128)S(1)}, f32[1,128,40]{1,2,0:T(8,128)}, u32[]{:S(2)}) copy-start(f32[1,128,40]{1,2,0:T(8,128)} %param.17) | copy-start | bytes 61444
  6.5 8.1 %copy-start.17 = (f32[40]{0:T(128)S(1)}, f32[40]{0:T(128)}, u32[]{:S(2)}) copy-start(f32[40]{0:T(128)} %param.18) | copy-start | bytes 484
  6.5 110.0 %all-gather.3.cloned.1.call-start = ((), (), s32[]{:S(2)}) async-start(), calls=%async_computation.3 | async-start | bytes 3686400 | tf_op jit(solution)/shard_map/all_gather | solution.py:55
  8.1 20.0 %collective-permute-start = (bf16[3,2688]{1,0:T(4,128)(2,1)}, bf16[3,2688]{1,0:T(4,128)(2,1)}, u32[]{:S(2)}, u32[]{:S(2)}) collective-permute-start(bf16[3,2688]{1,0:T(4,128)(2,1)} %slice_bitcast_fusion), channel_id=1, source_target_pairs={{0,8},{8,16},{16,24},{1,9},{9,17},{17,25},{2,10},{10,18},{18,26},{... | collective-permute-start | bytes 48392 | tf_op jit(solution)/shard_map/ppermute | solution.py:31
  34.5 7.4 %copy-start.7 = (f32[40,128]{1,0:T(8,128)S(1)}, f32[40,128]{1,0:T(8,128)}, u32[]{:S(2)}) copy-start(f32[40,128]{1,0:T(8,128)} %copy.75) | copy-start | bytes 61444
  34.6 7.4 %copy-start.8 = (f32[40,128]{1,0:T(8,128)S(1)}, f32[40,128]{1,0:T(8,128)}, u32[]{:S(2)}) copy-start(f32[40,128]{1,0:T(8,128)} %copy.73) | copy-start | bytes 61444
  34.6 7.4 %copy-start.9 = (pred[128,128]{1,0:T(8,128)(4,1)S(1)}, pred[128,128]{1,0:T(8,128)(4,1)}, u32[]{:S(2)}) copy-start(pred[128,128]{1,0:T(8,128)(4,1)} %iota_compare_fusion.5) | copy-start | bytes 49156
  35.0 8.2 %collective-permute-start.1 = (bf16[40,64,64]{2,1,0:T(8,128)(2,1)S(1)}, bf16[40,64,64]{2,1,0:T(8,128)(2,1)S(1)}, u32[]{:S(2)}, u32[]{:S(2)}) collective-permute-start(bf16[40,64,64]{2,1,0:T(8,128)(2,1)S(1)} %convolution_convert_fusion.2), channel_id=1, source_target_pairs={{0,8},{8,16},{16,24},{1,9},{9,17},{17,25},{2,10},{10,18},{18,26},{... | collective-permute-start | bytes 983048 | tf_op jit(solution)/shard_map/ppermute | solution.py:31
  37.1 18.5 %collective-permute-start.2 = (bf16[40,64,64]{2,1,0:T(8,128)(2,1)S(1)}, bf16[40,64,64]{2,1,0:T(8,128)(2,1)S(1)}, u32[]{:S(2)}, u32[]{:S(2)}) collective-permute-start(bf16[40,64,64]{2,1,0:T(8,128)(2,1)S(1)} %convolution_convert_fusion.2), channel_id=1, source_target_pairs={{0,16},{8,24},{1,17},{9,25},{2,18},{10,26},{3,19},{11,27},{4,20},{... | collective-permute-start | bytes 983048 | tf_op jit(solution)/shard_map/ppermute | solution.py:31
  40.5 26.3 %collective-permute-start.3 = (bf16[40,64,64]{2,1,0:T(8,128)(2,1)S(1)}, bf16[40,64,64]{2,1,0:T(8,128)(2,1)S(1)}, u32[]{:S(2)}, u32[]{:S(2)}) collective-permute-start(bf16[40,64,64]{2,1,0:T(8,128)(2,1)S(1)} %convolution_convert_fusion.2), channel_id=1, source_target_pairs={{0,24},{1,25},{2,26},{3,27},{4,28},{5,29},{6,30},{7,31}} | collective-permute-start | bytes 983048 | tf_op jit(solution)/shard_map/ppermute | solution.py:31
  42.0 24.8 %copy-start.4 = (f32[1,128,2560]{1,2,0:T(8,128)S(1)}, f32[1,128,2560]{1,2,0:T(8,128)}, u32[]{:S(2)}) copy-start(f32[1,128,2560]{1,2,0:T(8,128)} %copy.79) | copy-start | bytes 3932164
  42.0 24.8 %copy-start.14 = (f32[40]{0:T(128)S(1)}, f32[40]{0:T(128)}, u32[]{:S(2)}) copy-start(f32[40]{0:T(128)} %get-tuple-element.18) | copy-start | bytes 484
  42.0 24.8 %copy-start.15 = (f32[40]{0:T(128)S(1)}, f32[40]{0:T(128)}, u32[]{:S(2)}) copy-start(f32[40]{0:T(128)} %get-tuple-element.19) | copy-start | bytes 484
  42.0 24.8 %copy-start.18 = (f32[40]{0:T(128)S(1)}, f32[40]{0:T(128)}, u32[]{:S(2)}) copy-start(f32[40]{0:T(128)} %param.19) | copy-start | bytes 484
  71.6 23.2 %copy-start.12 = (s32[1,128,2]{1,2,0:T(2,128)S(1)}, s32[1,128,2]{1,2,0:T(2,128)}, u32[]{:S(2)}) copy-start(s32[1,128,2]{1,2,0:T(2,128)} %param.28) | copy-start | bytes 3076
  73.6 10.2 %collective-permute-start.4 = (bf16[128,2560]{1,0:T(8,128)(2,1)S(1)}, bf16[128,2560]{1,0:T(8,128)(2,1)S(1)}, u32[]{:S(2)}, u32[]{:S(2)}) collective-permute-start(bf16[128,2560]{1,0:T(8,128)(2,1)S(1)} %fusion.38), channel_id=1, source_target_pairs={{0,8},{8,16},{16,24},{24,0},{1,9},{9,17},{17,25},{25,1},{2,10},{10... | collective-permute-start | bytes 1966088 | tf_op jit(solution)/shard_map/ppermute | solution.py:17
  84.7 10.1 %collective-permute-start.5 = (bf16[128,2560]{1,0:T(8,128)(2,1)S(1)}, bf16[128,2560]{1,0:T(8,128)(2,1)}, u32[]{:S(2)}, u32[]{:S(2)}) collective-permute-start(bf16[128,2560]{1,0:T(8,128)(2,1)S(1)} %collective-permute-done.4), channel_id=1, source_target_pairs={{0,8},{8,16},{16,24},{24,0},{1,9},{9,17},{17,25},{25,1},{2,10},{10... | collective-permute-start | bytes 1966088 | tf_op jit(solution)/shard_map/ppermute | solution.py:17
  94.8 10.3 %collective-permute-start.6 = (bf16[128,2560]{1,0:T(8,128)(2,1)}, bf16[128,2560]{1,0:T(8,128)(2,1)}, u32[]{:S(2)}, u32[]{:S(2)}) collective-permute-start(bf16[128,2560]{1,0:T(8,128)(2,1)} %collective-permute-done.5), channel_id=1, source_target_pairs={{0,8},{8,16},{16,24},{24,0},{1,9},{9,17},{17,25},{25,1},{2,10},{10... | collective-permute-start | bytes 1966088 | tf_op jit(solution)/shard_map/ppermute | solution.py:17
  95.6 13.4 %copy-start.3 = (bf16[128,2560]{1,0:T(8,128)(2,1)S(1)}, bf16[128,2560]{1,0:T(8,128)(2,1)}, u32[]{:S(2)}) copy-start(bf16[128,2560]{1,0:T(8,128)(2,1)} %copy-done.2) | copy-start | bytes 1966084
  122.3 13.7 %all-to-all-start = ((bf16[4,128,640]{2,1,0:T(8,128)(2,1)}), bf16[4,128,640]{2,1,0:T(8,128)(2,1)S(1)}, u32[]{:S(2)}, u32[]{:S(2)}) async-start(bf16[4,128,640]{2,1,0:T(8,128)(2,1)} %bitcast.133), calls=%async_computation | async-start | bytes 1310720 | tf_op jit(solution)/shard_map/all_to_all | solution.py:120
  138.5 67.3 %copy-start.16 = (bf16[1,2560,512]{2,1,0:T(8,128)(2,1)S(1)}, bf16[1,2560,512]{2,1,0:T(8,128)(2,1)}, u32[]{:S(2)}) copy-start(bf16[1,2560,512]{2,1,0:T(8,128)(2,1)} %param.25) | copy-start | bytes 7864324
  215.5 4.9 %copy-start.13 = (f32[1,128,2]{1,2,0:T(2,128)S(1)}, f32[1,128,2]{1,2,0:T(2,128)}, u32[]{:S(2)}) copy-start(f32[1,128,2]{1,2,0:T(2,128)} %param.29) | copy-start | bytes 3076
  215.5 63.1 %all-to-all-start.2 = ((bf16[8,64,2560]{2,1,0:T(8,128)(2,1)}), bf16[8,64,2560]{2,1,0:T(8,128)(2,1)}, u32[]{:S(2)}, u32[]{:S(2)}) async-start(bf16[8,64,2560]{2,1,0:T(8,128)(2,1)} %bitcast.125), calls=%async_computation.2 | async-start | bytes 5242880 | tf_op jit(solution)/shard_map/all_to_all | solution.py:157
  (5 other events, 7.5 us)
Sparse Core Ops, SparseCore 0:
  13.0 63.9 all-gather.2
